TPU v7x, 256 devices: a whole 4x4x8 slice. The times are simulated.
256 devices in a mesh: row: 16 (over x, y), col: 16 (over z, core).
Axes of the slice: x: 4, y: 4, z: 8, core: 2. Of those that a mesh axis runs over, the one named last changes fastest.
Arguments:
- queries: bfloat16 [4096, 8192], P('col', 'row'), may hold values from -1 to 1
- passages: bfloat16 [4096, 8192], P('row', 'col'), may hold values from -1 to 1
- ce_scores: float32 [8192, 8192], P('row', 'col'), may hold values from -16 to 320
- colbert_scores: float32 [8192, 8192], P('row', 'col'), may hold values from -16 to 320
- mix: int32 [8192], P('row'), may hold values from 1 to 255
- positive: int32 [8192], P('row'), may hold values from 0 to 8191
Outputs:
- query_grad: bfloat16 [4096, 8192], P('col', 'row')
- passage_grad: bfloat16 [4096, 8192], P('row', 'col')
All inputs are finite; a program needn't handle non-finite values.
Results may differ from a plain program's by a relative error of at most 0.0044.
Values may be sent and summed in bfloat16 or wider, within the bound.
A program may use at most 64 MiB of HBM per device.

v0:
```python
import functools

import jax
import jax.numpy as jnp
from jax import lax
from jax.experimental import pallas as pl
from jax.experimental.pallas import tpu as pltpu
from jax.sharding import PartitionSpec as P

MESH = pl.DeviceIdType.MESH
DELTA = ((1, 0), (0, 1), (-1, 0), (0, -1))
LAG = 3
PIECES = 4


def far(offset):
    return sum(min(o, 4 - o) for o in offset)


def tree_edges(piece):
    base = [((0, 0), 0), ((1, 0), 0), ((0, 0), 2)]
    for x in range(4):
        base += [((x, 0), 1), ((x, 1), 1), ((x, 0), 3)]
    edges = []
    for (x, y), direction in base:
        for _ in range(piece):
            x, y = -y, x
        direction = (direction + piece) % 4
        dx, dy = DELTA[direction]
        edges.append(((x % 4, y % 4), direction, ((x + dx) % 4, (y + dy) % 4)))
    return edges


def xy_schedule():
    trees = [tree_edges(piece) for piece in range(PIECES)]

    def weight(piece, node):
        below = [weight(piece, to) for start, _, to in trees[piece] if start == node]
        return (1 + max(b[0] for b in below), 1 + sum(b[1] for b in below)) if below else (0, 1)

    ready = {(piece, (0, 0)): 0 for piece in range(PIECES)}
    left = {(piece,) + edge for piece in range(PIECES) for edge in trees[piece]}
    plan = [[] for _ in range(4)]
    slot = 0
    while left:
        taken = []
        for direction in range(4):
            able = [e for e in left if e[2] == direction and ready.get((e[0], e[1]), 99) <= slot]
            if able:
                able.sort(key=lambda e: (-far(e[3]), weight(e[0], e[3]), -((e[0] - direction) % 4)), reverse=True)
                taken.append(able[0])
        for piece, start, direction, to in taken:
            left.remove((piece, start, direction, to))
            plan[direction].append((piece, start, to))
            ready[piece, to] = slot + LAG
        slot += 1
    return plan


GATHER_XY = xy_schedule()
REDUCE_XY = [[(p, to, start) for p, start, to in reversed(GATHER_XY[(d + 2) % 4])] for d in range(4)]
HALVES = ((0, 1, 2, 3), (2, 3, 0, 1))
GATHER_Z = [
    [(k, u, False) for k in range(3) for u in h] + [(3, h[0], False), (3, h[1], False), (3, h[1], True)]
    for h in HALVES
]
REDUCE_Z = [
    [(4, h[1], False), (4, h[1], True), (4, h[0], False)]
    + [(k, u, False) for k in (3, 2, 1) for u in (h[2], h[3], h[1], h[0])]
    for h in HALVES
]
FAR_PAIR = [h[0] for h in HALVES]
SLOTS_XY = len(GATHER_XY[0])
SLOTS_Z = len(GATHER_Z[0])
OFFSETS = [(x, y) for x in range(4) for y in range(4)]


def pick(index, values):
    out = jnp.int32(values[0])
    for at, value in enumerate(values[1:], 1):
        out = jnp.where(index == at, jnp.int32(value), out)
    return out


def kernel(
    q_hbm, p_hbm, ce_hbm, cb_hbm, mix_hbm, pos_hbm,
    out_ref,
    q_all, p_all, ce_v, cb_v, mix_ref, pos_ref, s_acc, t_acc, gs_t, st_s, st_t,
    pg_acc, qg_acc, pair_out, pair_in, xy_out, xy_in, z_out, z_in,
    local_sem, send_sem, gxy_sem, gz_sem, gpair_sem, st_sem, rxy_sem, rz_sem, rpair_sem,
):
    row, col = lax.axis_index("row"), lax.axis_index("col")
    x, y, z, core = row // 4, row % 4, col // 2, col % 2
    depth, width = q_hbm.shape
    unit = depth // PIECES

    def row_at(dx, dy):
        return ((x + dx + 4) % 4) * 4 + (y + dy + 4) % 4

    def z_at(dz):
        return (z + dz + 8) % 8

    xy_dev = [(row_at(dx, dy), col) for dx, dy in DELTA]
    z_dev = [(row, z_at(1) * 2 + core), (row, z_at(-1) * 2 + core)]
    cross_dev = [(row, z_at(1) * 2 + 1 - core), (row, z_at(-1) * 2 + 1 - core)]
    pair_dev = (row, z * 2 + 1 - core)

    def shard(ref, index):
        return ref.at[pl.ds(pl.multiple_of(index * depth, depth), depth)]

    def piece(ref, index, u):
        return ref.at[pl.ds(pl.multiple_of(index * depth + u * unit, unit), unit)]

    def remote(src, dst, ssem, rsem, dev):
        return pltpu.make_async_remote_copy(
            src_ref=src, dst_ref=dst, send_sem=ssem, recv_sem=rsem, device_id=dev, device_id_type=MESH
        )

    barrier = pltpu.get_barrier_semaphore()
    for dev in xy_dev + z_dev + [pair_dev]:
        pl.semaphore_signal(barrier, inc=1, device_id=dev, device_id_type=MESH)
    loads = [
        pltpu.make_async_copy(src, dst, local_sem.at[at])
        for at, (src, dst) in enumerate(
            (
                (q_hbm, shard(q_all, col)),
                (p_hbm, shard(p_all, row)),
                (ce_hbm, ce_v),
                (cb_hbm, cb_v),
                (mix_hbm, mix_ref),
                (pos_hbm, pos_ref),
            )
        )
    ]
    for load in loads:
        load.start()
    pl.semaphore_wait(barrier, 7)

    def row_from(off):
        return row_at(-off[0], -off[1])

    def gxy_copy(d, t):
        p, start, _ = GATHER_XY[d][t]
        ref = piece(p_all, row_from(start), p)
        src = p_hbm.at[pl.ds(p * unit, unit)] if start == (0, 0) else ref
        return remote(src, ref, send_sem.at[d], gxy_sem.at[d * SLOTS_XY + t], xy_dev[d])

    def gxy_wait(d, t):
        p, _, to = GATHER_XY[d][t]
        ref = piece(p_all, row_from(to), p)
        remote(ref, ref, send_sem.at[d], gxy_sem.at[d * SLOTS_XY + t], xy_dev[d]).wait_recv()

    def z_from(d, k, core_of):
        return z_at(-k if d == 0 else k) * 2 + core_of

    def gz_copy(d, t):
        k, u, cross = GATHER_Z[d][t]
        ref = piece(q_all, z_from(d, k, core), u)
        src = q_hbm.at[pl.ds(u * unit, unit)] if k == 0 else ref
        dev = cross_dev[d] if cross else z_dev[d]
        return remote(src, ref, send_sem.at[4 + d], gz_sem.at[d * SLOTS_Z + t], dev)

    def gz_wait(d, t):
        k, u, cross = GATHER_Z[d][t]
        ref = piece(q_all, z_from(d, k + 1, 1 - core if cross else core), u)
        dev = cross_dev[d] if cross else z_dev[d]
        remote(ref, ref, send_sem.at[4 + d], gz_sem.at[d * SLOTS_Z + t], dev).wait_recv()
        offset = (k + 1) if d == 1 else (8 - k - 1)
        if k < 3:
            remote(ref, ref, send_sem.at[6], gpair_sem.at[offset], pair_dev).start()
        elif u == FAR_PAIR[d]:
            remote(ref, ref, send_sem.at[6], gpair_sem.at[8 * d], pair_dev).start()

    def gpair_wait(offset):
        other = z_at(offset) * 2 + 1 - core
        if offset == 4:
            for d in range(2):
                ref = piece(q_all, other, FAR_PAIR[d])
                remote(ref, ref, send_sem.at[6], gpair_sem.at[8 * d], pair_dev).wait_recv()
        else:
            ref = shard(q_all, other)
            at = 4 if offset == 0 else offset
            remote(ref, ref, send_sem.at[6], gpair_sem.at[at], pair_dev).wait_recv()

    last_step = SLOTS_XY + LAG - 1
    p_steps = [0] * 5
    for d in range(4):
        for t, (_, _, to) in enumerate(GATHER_XY[d]):
            p_steps[far(to)] = max(p_steps[far(to)], t + LAG)
    z_steps = [0] * 5
    for d in range(2):
        for t, (k, _, cross) in enumerate(GATHER_Z[d]):
            z_steps[k + 1] = max(z_steps[k + 1], t + LAG - (1 if cross else 0))

    s_acc[...] = jnp.zeros_like(s_acc)

    def add_scores(lo, hi):
        def body(i, carry):
            dx, dy, dz = jnp.abs(x - i // 4), jnp.abs(y - i % 4), jnp.abs(z - i // 2)
            p_far = jnp.minimum(dx, 4 - dx) + jnp.minimum(dy, 4 - dy)
            z_far = jnp.minimum(dz, 8 - dz)
            other = jnp.where(i % 2 == core, 0, 1)
            at = jnp.maximum(pick(p_far, p_steps), pick(z_far, z_steps) + other)

            @pl.when(jnp.logical_and(at >= lo, at <= hi))
            def _():
                start = pl.multiple_of(i * depth, depth)
                s_acc[...] += lax.dot_general(
                    p_all[pl.ds(start, depth), :],
                    q_all[pl.ds(start, depth), :],
                    (((0,), (0,)), ((), ())),
                    preferred_element_type=jnp.float32,
                )

            return carry

        lax.fori_loop(0, 16, body, 0)

    def teacher():
        for load in loads:
            load.wait()
        share = mix_ref[...].astype(jnp.float32) / 256.0
        top = jnp.full((1, width), -jnp.inf, jnp.float32)
        for b in range(width // 128):
            lanes = pl.ds(b * 128, 128)
            t = share * ce_v[:, lanes].T + (1.0 - share) * cb_v[:, lanes].T
            t_acc[lanes, :] = t
            top = jnp.maximum(top, jnp.max(t, axis=0, keepdims=True))
        return top

    rows_at_once = 32
    blocks = width // rows_at_once

    def exp_sum(ref, top, scale):
        def body(b, total):
            rows = pl.ds(pl.multiple_of(b * rows_at_once, rows_at_once), rows_at_once)
            e = jnp.exp((ref[rows, :] - top) * scale)
            ref[rows, :] = e
            return total + jnp.sum(e.reshape(rows_at_once // 8, 8, width), axis=0)

        total = lax.fori_loop(0, blocks, body, jnp.zeros((8, width), jnp.float32))
        return jnp.sum(total, axis=0, keepdims=True)

    def put_stats(ref, top, total):
        for k in range(width // 128):
            ref[col, pl.ds(k, 1), :] = top[:, k * 128:(k + 1) * 128]
            ref[col, pl.ds(4 + k, 1), :] = total[:, k * 128:(k + 1) * 128]

    def send_stats(ref, which):
        def body(j, carry):
            k = 8 + ((j + 1) // 2) * (1 - 2 * (j % 2))
            to = (col + k) % 16
            remote(
                ref.at[col], ref.at[col], send_sem.at[7 + which], st_sem.at[which * 16 + k], (row, to)
            ).start()
            return carry

        lax.fori_loop(0, 15, body, 0)

    def wait_stats(ref, which):
        def body(k, carry):
            src = (col - k + 16) % 16
            remote(
                ref.at[src], ref.at[src], send_sem.at[7 + which], st_sem.at[which * 16 + k], (row, src)
            ).wait_recv()
            return carry

        lax.fori_loop(1, 16, body, 0)

    def combine(ref, scale):
        everyone = ref[...]
        tops, totals = everyone[:, 0:4, :], everyone[:, 4:8, :]
        top = jnp.max(tops, axis=0)
        total = jnp.sum(totals * jnp.exp((tops - top[None]) * scale), axis=0)
        mine = ref[col]
        return jnp.exp((mine[0:4, :] - top) * scale) / total

    computed = 0
    for t in range(last_step + 1):
        for d in range(4):
            if 0 <= t - LAG < SLOTS_XY:
                gxy_wait(d, t - LAG)
        for d in range(2):
            if 0 <= t - LAG < SLOTS_Z:
                gz_wait(d, t - LAG)
        for d in range(2):
            if t < SLOTS_Z:
                gz_copy(d, t).start()
        for d in range(4):
            if t < SLOTS_XY:
                gxy_copy(d, t).start()
        if t == 0:
            remote(q_hbm, shard(q_all, col), send_sem.at[6], gpair_sem.at[4], pair_dev).start()
        if t == LAG:
            gpair_wait(0)
        for offset in range(1, 8):
            if z_steps[min(offset, 8 - offset)] + 1 == t:
                gpair_wait(offset)
        if t == 2:
            t_top = teacher()
            t_total = exp_sum(t_acc, t_top, 1.0)
            put_stats(st_t, t_top, t_total)
        if t == last_step:
            send_stats(st_t, 1)
        if t in (7, 10, 11, 12, 14, 15, 16, last_step):
            add_scores(computed, t)
            computed = t + 1

    def max_body(b, top):
        rows = pl.ds(pl.multiple_of(b * rows_at_once, rows_at_once), rows_at_once)
        return jnp.maximum(top, jnp.max(s_acc[rows, :].reshape(rows_at_once // 8, 8, width), axis=0))

    s_top = lax.fori_loop(0, blocks, max_body, jnp.full((8, width), -jnp.inf, jnp.float32))
    s_top = jnp.max(s_top, axis=0, keepdims=True)
    s_total = exp_sum(s_acc, s_top, 20.0)
    put_stats(st_s, s_top, s_total)
    send_stats(st_s, 0)

    wait_stats(st_t, 1)
    t_scale = combine(st_t, 1.0) * -20.0
    target = pos_ref[...] - col * width

    def teacher_body(b, carry):
        start = pl.multiple_of(b * rows_at_once, rows_at_once)
        rows = pl.ds(start, rows_at_once)
        scale = jnp.concatenate([t_scale[k:k + 1, :] for k in range(4)], axis=1)
        index = lax.broadcasted_iota(jnp.int32, (rows_at_once, width), 0) + start
        t_acc[rows, :] = t_acc[rows, :] * scale - jnp.where(index == target, 10.0, 0.0)
        return carry

    lax.fori_loop(0, blocks, teacher_body, 0)

    wait_stats(st_s, 0)
    s_scale = combine(st_s, 20.0) * 30.0

    def grad_body(b, carry):
        rows = pl.ds(pl.multiple_of(b * rows_at_once, rows_at_once), rows_at_once)
        scale = jnp.concatenate([s_scale[k:k + 1, :] for k in range(4)], axis=1)
        gs_t[rows, :] = (s_acc[rows, :] * scale + t_acc[rows, :]).astype(jnp.bfloat16)
        return carry

    lax.fori_loop(0, blocks, grad_body, 0)

    def query_part(offset, core_of):
        lhs = shard(p_all, z_at(offset) * 2 + core_of)[...]
        return jnp.dot(lhs, gs_t[...], preferred_element_type=jnp.float32)

    def pair_copies(offset):
        if offset != 4:
            whole = pair_out.at[offset], pair_in.at[offset]
            return [remote(*whole, send_sem.at[15], rpair_sem.at[offset], pair_dev)]
        return [
            remote(
                pair_out.at[4, pl.ds(u * unit, unit)], pair_in.at[4, pl.ds(u * unit, unit)],
                send_sem.at[15], rpair_sem.at[4 + 4 * at], pair_dev,
            )
            for at, u in enumerate(FAR_PAIR)
        ]

    def query_pair(offset):
        pair_out[offset] = query_part(offset, 1 - core).astype(jnp.bfloat16)
        for copy in pair_copies(offset):
            copy.start()

    def query_own(offset):
        qg_acc[offset] = query_part(offset, core)
        if offset != 4:
            pair_copies(offset)[0].wait_recv()

    passage_done = set()

    def passage_part(off):
        if off not in passage_done:
            passage_done.add(off)
            lhs = shard(q_all, row_from(off))[...]
            pg_acc[OFFSETS.index(off)] = lax.dot_general(
                lhs, gs_t[...], (((1,), (1,)), ((), ())), preferred_element_type=jnp.float32
            )

    def rxy_copy(d, t):
        return remote(
            xy_out.at[d * SLOTS_XY + t], xy_in.at[d * SLOTS_XY + t], send_sem.at[9 + d],
            rxy_sem.at[d * SLOTS_XY + t], xy_dev[d],
        )

    def xy_sum(p, off):
        total = pg_acc[OFFSETS.index(off), pl.ds(p * unit, unit), :]
        for d in range(4):
            for t, (p2, _, to) in enumerate(REDUCE_XY[d]):
                if p2 == p and to == off:
                    rxy_copy(d, t).wait_recv()
                    total += xy_in[d * SLOTS_XY + t].astype(jnp.float32)
        return total

    def rz_copy(d, t):
        _, u, cross = REDUCE_Z[d][t]
        src = pair_out.at[4, pl.ds(u * unit, unit)] if cross else z_out.at[d * SLOTS_Z + t]
        dev = cross_dev[d] if cross else z_dev[d]
        return remote(src, z_in.at[d * SLOTS_Z + t], send_sem.at[13 + d], rz_sem.at[d * SLOTS_Z + t], dev)

    def z_sum(directions, k, u):
        offset = (k if directions[0] == 0 else 8 - k) % 8
        rows = pl.ds(u * unit, unit)
        total = qg_acc[offset, rows, :]
        if k < 4:
            total += pair_in[offset, rows, :].astype(jnp.float32)
        elif u == FAR_PAIR[directions[0]]:
            pair_copies(4)[directions[0]].wait_recv()
            total += pair_in[offset, rows, :].astype(jnp.float32)
        for d in directions:
            for t, (k2, u2, _) in enumerate(REDUCE_Z[d]):
                if (k2, u2) == (k + 1, u):
                    rz_copy(d, t).wait_recv()
                    total += z_in[d * SLOTS_Z + t].astype(jnp.float32)
        return total

    query_pair(4)
    passage_part((2, 2))
    query_own(4)
    for t in range(SLOTS_XY):
        for d in range(4):
            p, off, _ = REDUCE_XY[d][t]
            passage_part(off)
            xy_out[d * SLOTS_XY + t] = xy_sum(p, off).astype(jnp.bfloat16)
            rxy_copy(d, t).start()
        for d in range(2):
            k, u, cross = REDUCE_Z[d][t]
            if not cross:
                z_out[d * SLOTS_Z + t] = z_sum((d,), k, u).astype(jnp.bfloat16)
            rz_copy(d, t).start()
        for at, offset in ((0, 3), (0, 5), (3, 2), (3, 6), (7, 1), (7, 7), (10, 0)):
            if t == at:
                query_pair(offset)
            if t == at + 1:
                query_own(offset)
    passage_part((0, 0))
    for u in range(PIECES):
        rows = pl.ds(u * unit, unit)
        out_ref[pl.ds(depth + u * unit, unit), :] = xy_sum(u, (0, 0)).astype(jnp.bfloat16)
        out_ref[rows, :] = z_sum((0, 1), 0, u).astype(jnp.bfloat16)

    def sent(ref, sem, dev):
        remote(ref, ref, sem, sem, dev).wait_send()

    for d in range(4):
        sent(p_all.at[pl.ds(0, SLOTS_XY * unit)], send_sem.at[d], xy_dev[d])
        sent(xy_out.at[pl.ds(d * SLOTS_XY, SLOTS_XY)], send_sem.at[9 + d], xy_dev[d])
    for d in range(2):
        sent(q_all.at[pl.ds(0, SLOTS_Z * unit)], send_sem.at[4 + d], z_dev[d])
        sent(z_out.at[pl.ds(d * SLOTS_Z, SLOTS_Z)], send_sem.at[13 + d], z_dev[d])
    sent(q_all.at[pl.ds(0, 30 * unit)], send_sem.at[6], pair_dev)
    sent(q_all.at[pl.ds(0, 30 * unit)], send_sem.at[15], pair_dev)
    sent(st_s.at[pl.ds(0, 15)], send_sem.at[7], pair_dev)
    sent(st_t.at[pl.ds(0, 15)], send_sem.at[8], pair_dev)


def per_device(queries, passages, ce_scores, colbert_scores, mix, positive):
    depth, width = queries.shape
    unit = depth // PIECES
    bf16, f32 = jnp.bfloat16, jnp.float32
    hbm = pl.BlockSpec(memory_space=pl.ANY)
    vmem = pl.BlockSpec(memory_space=pltpu.VMEM)
    out = pltpu.VMEM((2 * depth, width), bf16)
    dma = pltpu.SemaphoreType.DMA
    grads = pl.pallas_call(
        kernel,
        out_shape=out,
        in_specs=[hbm] * 6,
        out_specs=vmem,
        scratch_shapes=[
            pltpu.VMEM((16 * depth, width), bf16),
            pltpu.VMEM((16 * depth, width), bf16),
            pltpu.VMEM((width, width), f32),
            pltpu.VMEM((width, width), f32),
            pltpu.VMEM((1, width), jnp.int32),
            pltpu.VMEM((1, width), jnp.int32),
            pltpu.VMEM((width, width), f32),
            pltpu.VMEM((width, width), f32),
            pltpu.VMEM((width, width), bf16),
            pltpu.VMEM((16, 8, 128), f32),
            pltpu.VMEM((16, 8, 128), f32),
            pltpu.VMEM((16, depth, width), f32),
            pltpu.VMEM((8, depth, width), f32),
            pltpu.VMEM((8, depth, width), bf16),
            pltpu.VMEM((8, depth, width), bf16),
            pltpu.VMEM((4 * SLOTS_XY, unit, width), bf16),
            pltpu.VMEM((4 * SLOTS_XY, unit, width), bf16),
            pltpu.VMEM((2 * SLOTS_Z, unit, width), bf16),
            pltpu.VMEM((2 * SLOTS_Z, unit, width), bf16),
            dma((6,)),
            dma((16,)),
            dma((4 * SLOTS_XY,)),
            dma((2 * SLOTS_Z,)),
            dma((9,)),
            dma((32,)),
            dma((4 * SLOTS_XY,)),
            dma((2 * SLOTS_Z,)),
            dma((9,)),
        ],
        compiler_params=pltpu.CompilerParams(collective_id=0, has_side_effects=True),
    )(queries, passages, ce_scores, colbert_scores, mix.reshape(1, width), positive.reshape(1, width))
    return grads[:depth], grads[depth:]


def solution(mesh):
    in_specs = (
        P("col", "row"),
        P("row", "col"),
        P("row", "col"),
        P("row", "col"),
        P("row"),
        P("row"),
    )
    out_specs = (P("col", "row"), P("row", "col"))
    return jax.shard_map(
        per_device, mesh=mesh, in_specs=in_specs, out_specs=out_specs, check_vma=False
    )
```

profile of v0, /device:TPU:1, one launch (start us, length us, event | category | flops | bytes accessed | tf_op | source)
XLA Modules:
  0.0 70.8 jit_solution(10441234563559372736)
XLA Ops:
  0.6 69.3 %shard_map.77 = bf16[512,512]{1,0:T(8,128)(2,1)S(1)} custom-call(bf16[256,512]{1,0:T(8,128)(2,1)} %q_hbm.1, bf16[256,512]{1,0:T(8,128)(2,1)} %p_hbm.1, f32[512,512]{1,0:T(8,128)} %ce_hbm.1, f32[512,512]{1,0:T(8,128)} %cb_hbm.1, s32[1,512]{1,0:T(1,128)} %bitcast.2, s32[1,512]{1,0:T(1,128)} %bitcast.3), custom_call_target="tpu_custom_call" | custom-call | tf_op jit(solution)/shard_map/pallas_call | solution.py:465
  70.0 0.8 %fusion = (bf16[256,512]{1,0:T(8,128)(2,1)}, bf16[256,512]{1,0:T(8,128)(2,1)}) fusion(bf16[512,512]{1,0:T(8,128)(2,1)S(1)} %shard_map.77), kind=kLoop, calls=%fused_computation | loop fusion | bytes 1048576 | tf_op jit(solution)/shard_map/slice | solution.py:502
where the time goes:
time: 70.9 us; the launch traced here: 70.8 us
  Pallas kernels  69.3 us (98%)
  local copies, waits for them, and re-layouts  0.82 us (1%)
    pallas_call x1, Pallas kernels, per_device(): pl.pallas_call(kernel, out_shape=out, in_specs=[hbm] * 6, out_specs=vmem,...  69.3 us

commit v1 on v0

--- a/solution.py
+++ b/solution.py
@@ -9,12 +9,22 @@
 
 MESH = pl.DeviceIdType.MESH
 DELTA = ((1, 0), (0, 1), (-1, 0), (0, -1))
-LAG = 3
+LAG = 4
 PIECES = 4
 
 
 def far(offset):
     return sum(min(o, 4 - o) for o in offset)
+
+
+def group(offset):
+    two_x, two_y = offset[0] == 2, offset[1] == 2
+    if far(offset) == 3:
+        return 5 if two_x else 3
+    return 6 if far(offset) == 2 and (two_x or two_y) else far(offset)
+
+
+TURNS = {(2, 0): 0, (0, 2): 0, (1, 1): 1, (3, 3): 1, (3, 1): 2, (1, 3): 2, (1, 2): 0, (3, 2): 0, (2, 1): 1, (2, 3): 1}
 
 
 def tree_edges(piece):
@@ -34,9 +44,8 @@
 def xy_schedule():
     trees = [tree_edges(piece) for piece in range(PIECES)]
 
-    def weight(piece, node):
-        below = [weight(piece, to) for start, _, to in trees[piece] if start == node]
-        return (1 + max(b[0] for b in below), 1 + sum(b[1] for b in below)) if below else (0, 1)
+    def late(piece, node):
+        return far(node) == 3 and all(start != node for start, _, _ in trees[piece])
 
     ready = {(piece, (0, 0)): 0 for piece in range(PIECES)}
     left = {(piece,) + edge for piece in range(PIECES) for edge in trees[piece]}
@@ -47,7 +56,7 @@
         for direction in range(4):
             able = [e for e in left if e[2] == direction and ready.get((e[0], e[1]), 99) <= slot]
             if able:
-                able.sort(key=lambda e: (-far(e[3]), weight(e[0], e[3]), -((e[0] - direction) % 4)), reverse=True)
+                able.sort(key=lambda e: (far(e[3]), late(e[0], e[3]), TURNS.get(e[3], (0, 2, 3, 1)[(e[0] - direction) % 4])))
                 taken.append(able[0])
         for piece, start, direction, to in taken:
             left.remove((piece, start, direction, to))
@@ -183,21 +192,23 @@
             remote(ref, ref, send_sem.at[6], gpair_sem.at[at], pair_dev).wait_recv()
 
     last_step = SLOTS_XY + LAG - 1
-    p_steps = [0] * 5
+    p_steps = [0] * 7
     for d in range(4):
         for t, (_, _, to) in enumerate(GATHER_XY[d]):
-            p_steps[far(to)] = max(p_steps[far(to)], t + LAG)
+            p_steps[group(to)] = max(p_steps[group(to)], t + LAG)
     z_steps = [0] * 5
     for d in range(2):
         for t, (k, _, cross) in enumerate(GATHER_Z[d]):
             z_steps[k + 1] = max(z_steps[k + 1], t + LAG - (1 if cross else 0))
 
-    s_acc[...] = jnp.zeros_like(s_acc)
 
     def add_scores(lo, hi):
         def body(i, carry):
             dx, dy, dz = jnp.abs(x - i // 4), jnp.abs(y - i % 4), jnp.abs(z - i // 2)
-            p_far = jnp.minimum(dx, 4 - dx) + jnp.minimum(dy, 4 - dy)
+            dx, dy = jnp.minimum(dx, 4 - dx), jnp.minimum(dy, 4 - dy)
+            p_far = dx + dy
+            two = jnp.where(p_far == 2, jnp.maximum(dx, dy), 0) == 2
+            p_far = jnp.where(two, 6, jnp.where(jnp.where(p_far == 3, dx, 0) == 2, 5, p_far))
             z_far = jnp.minimum(dz, 8 - dz)
             other = jnp.where(i % 2 == core, 0, 1)
             at = jnp.maximum(pick(p_far, p_steps), pick(z_far, z_steps) + other)
@@ -228,7 +239,7 @@
             top = jnp.maximum(top, jnp.max(t, axis=0, keepdims=True))
         return top
 
-    rows_at_once = 32
+    rows_at_once = 64
     blocks = width // rows_at_once
 
     def exp_sum(ref, top, scale):
@@ -275,20 +286,31 @@
         mine = ref[col]
         return jnp.exp((mine[0:4, :] - top) * scale) / total
 
+    arrives = {(p, to): (d, t) for d in range(4) for t, (p, _, to) in enumerate(GATHER_XY[d])}
+    waited = set()
+
+    def here(wait, d, t):
+        if (wait, d, t) not in waited:
+            waited.add((wait, d, t))
+            wait(d, t)
+
     computed = 0
     for t in range(last_step + 1):
+        for slot in range(4) if t == 0 else (t,) if 4 <= t < SLOTS_XY else ():
+            for d in range(2):
+                if slot >= 4:
+                    here(gz_wait, d, GATHER_Z[d].index((GATHER_Z[d][slot][0] - 1, GATHER_Z[d][slot][1], False)))
+                gz_copy(d, slot).start()
+            for d in range(4):
+                if slot >= 4:
+                    here(gxy_wait, *arrives[GATHER_XY[d][slot][:2]])
+                gxy_copy(d, slot).start()
+        for d in range(2):
+            if 0 <= t - LAG < SLOTS_Z:
+                here(gz_wait, d, t - LAG)
         for d in range(4):
             if 0 <= t - LAG < SLOTS_XY:
-                gxy_wait(d, t - LAG)
-        for d in range(2):
-            if 0 <= t - LAG < SLOTS_Z:
-                gz_wait(d, t - LAG)
-        for d in range(2):
-            if t < SLOTS_Z:
-                gz_copy(d, t).start()
-        for d in range(4):
-            if t < SLOTS_XY:
-                gxy_copy(d, t).start()
+                here(gxy_wait, d, t - LAG)
         if t == 0:
             remote(q_hbm, shard(q_all, col), send_sem.at[6], gpair_sem.at[4], pair_dev).start()
         if t == LAG:
@@ -296,13 +318,14 @@
         for offset in range(1, 8):
             if z_steps[min(offset, 8 - offset)] + 1 == t:
                 gpair_wait(offset)
-        if t == 2:
+        if t == 0:
+            s_acc[...] = jnp.zeros_like(s_acc)
             t_top = teacher()
             t_total = exp_sum(t_acc, t_top, 1.0)
             put_stats(st_t, t_top, t_total)
         if t == last_step:
             send_stats(st_t, 1)
-        if t in (7, 10, 11, 12, 14, 15, 16, last_step):
+        if t in (8, 11, 12, 13, 15, 16, 17, last_step):
             add_scores(computed, t)
             computed = t + 1
 
@@ -364,8 +387,8 @@
 
     def query_own(offset):
         qg_acc[offset] = query_part(offset, core)
-        if offset != 4:
-            pair_copies(offset)[0].wait_recv()
+
+    paired = set()
 
     passage_done = set()
 
@@ -403,6 +426,9 @@
         rows = pl.ds(u * unit, unit)
         total = qg_acc[offset, rows, :]
         if k < 4:
+            if offset not in paired:
+                paired.add(offset)
+                pair_copies(offset)[0].wait_recv()
             total += pair_in[offset, rows, :].astype(jnp.float32)
         elif u == FAR_PAIR[directions[0]]:
             pair_copies(4)[directions[0]].wait_recv()

time: 70.9 us -> 68.8 us (0.970)
  Pallas kernels: 69.3 us -> 67.2 us
    pallas_call x1, Pallas kernels: 69.3 us -> 67.2 us  [per_device(): pl.pallas_call(kernel, out_shape=out, in_specs=[hbm] * 6, out_specs=vmem,...]
where the time goes in v1:
time: 68.8 us; the launch traced here: 68.7 us
  Pallas kernels  67.2 us (98%)
  local copies, waits for them, and re-layouts  0.82 us (1%)
    pallas_call x1, Pallas kernels, per_device(): pl.pallas_call(kernel, out_shape=out, in_specs=[hbm] * 6, out_specs=vmem,...  67.2 us

profile of v1, /device:TPU:1, one launch (start us, length us, event | category | flops | bytes accessed | tf_op | source)
XLA Modules:
  0.0 68.7 jit_solution(2991811675172079318)
XLA Ops:
  0.6 67.2 %shard_map.77 = bf16[512,512]{1,0:T(8,128)(2,1)S(1)} custom-call(bf16[256,512]{1,0:T(8,128)(2,1)} %q_hbm.1, bf16[256,512]{1,0:T(8,128)(2,1)} %p_hbm.1, f32[512,512]{1,0:T(8,128)} %ce_hbm.1, f32[512,512]{1,0:T(8,128)} %cb_hbm.1, s32[1,512]{1,0:T(1,128)} %bitcast.2, s32[1,512]{1,0:T(1,128)} %bitcast.3), custom_call_target="tpu_custom_call" | custom-call | tf_op jit(solution)/shard_map/pallas_call | solution.py:491
  67.9 0.8 %fusion = (bf16[256,512]{1,0:T(8,128)(2,1)}, bf16[256,512]{1,0:T(8,128)(2,1)}) fusion(bf16[512,512]{1,0:T(8,128)(2,1)S(1)} %shard_map.77), kind=kLoop, calls=%fused_computation | loop fusion | bytes 1048576 | tf_op jit(solution)/shard_map/slice | solution.py:528

commit v2 on v1

--- a/solution.py
+++ b/solution.py
@@ -202,6 +202,15 @@
             z_steps[k + 1] = max(z_steps[k + 1], t + LAG - (1 if cross else 0))
 
 
+    def add_chunk(i):
+        start = pl.multiple_of(i * depth, depth)
+        s_acc[...] += lax.dot_general(
+            p_all[pl.ds(start, depth), :],
+            q_all[pl.ds(start, depth), :],
+            (((0,), (0,)), ((), ())),
+            preferred_element_type=jnp.float32,
+        )
+
     def add_scores(lo, hi):
         def body(i, carry):
             dx, dy, dz = jnp.abs(x - i // 4), jnp.abs(y - i % 4), jnp.abs(z - i // 2)
@@ -215,13 +224,7 @@
 
             @pl.when(jnp.logical_and(at >= lo, at <= hi))
             def _():
-                start = pl.multiple_of(i * depth, depth)
-                s_acc[...] += lax.dot_general(
-                    p_all[pl.ds(start, depth), :],
-                    q_all[pl.ds(start, depth), :],
-                    (((0,), (0,)), ((), ())),
-                    preferred_element_type=jnp.float32,
-                )
+                add_chunk(i)
 
             return carry
 
@@ -325,7 +328,16 @@
             put_stats(st_t, t_top, t_total)
         if t == last_step:
             send_stats(st_t, 1)
-        if t in (8, 11, 12, 13, 15, 16, 17, last_step):
+        if t == last_step:
+            assert p_steps[4] == z_steps[4] + 1 == t > max(p_steps[:4] + p_steps[5:] + z_steps)
+            first, second = row_from((2, 2)), z_at(4) * 2 + 1 - core
+            add_chunk(first)
+
+            @pl.when(first != second)
+            def _():
+                add_chunk(second)
+
+        if t in (8, 11, 12, 13, 15, 16, 17):
             add_scores(computed, t)
             computed = t + 1
 
@@ -440,26 +452,28 @@
                     total += z_in[d * SLOTS_Z + t].astype(jnp.float32)
         return total
 
-    query_pair(4)
-    passage_part((2, 2))
-    query_own(4)
     for t in range(SLOTS_XY):
         for d in range(4):
             p, off, _ = REDUCE_XY[d][t]
             passage_part(off)
             xy_out[d * SLOTS_XY + t] = xy_sum(p, off).astype(jnp.bfloat16)
             rxy_copy(d, t).start()
+        if t == 0:
+            query_own(4)
         for d in range(2):
             k, u, cross = REDUCE_Z[d][t]
             if not cross:
                 z_out[d * SLOTS_Z + t] = z_sum((d,), k, u).astype(jnp.bfloat16)
             rz_copy(d, t).start()
-        for at, offset in ((0, 3), (0, 5), (3, 2), (3, 6), (7, 1), (7, 7), (10, 0)):
+        if t == 0:
+            query_pair(4)
+        if t == 12:
+            passage_part((0, 0))
+        for at, offset in ((1, 3), (1, 5), (4, 2), (4, 6), (8, 1), (8, 7), (11, 0)):
             if t == at:
                 query_pair(offset)
             if t == at + 1:
                 query_own(offset)
-    passage_part((0, 0))
     for u in range(PIECES):
         rows = pl.ds(u * unit, unit)
         out_ref[pl.ds(depth + u * unit, unit), :] = xy_sum(u, (0, 0)).astype(jnp.bfloat16)

time: 68.8 us -> 68 us (0.988)
  Pallas kernels: 67.2 us -> 66.5 us
    pallas_call x1, Pallas kernels: 67.2 us -> 66.5 us  [per_device(): pl.pallas_call(kernel, out_shape=out, in_specs=[hbm] * 6, out_specs=vmem,...]
where the time goes in v2:
time: 68 us; the launch traced here: 67.9 us
  Pallas kernels  66.5 us (98%)
  local copies, waits for them, and re-layouts  0.82 us (1%)
    pallas_call x1, Pallas kernels, per_device(): pl.pallas_call(kernel, out_shape=out, in_specs=[hbm] * 6, out_specs=vmem,...  66.5 us

profile of v2, /device:TPU:1, one launch (start us, length us, event | category | flops | bytes accessed | tf_op | source)
XLA Modules:
  0.0 67.9 jit_solution(12519484625233563361)
XLA Ops:
  0.6 66.5 %shard_map.77 = bf16[512,512]{1,0:T(8,128)(2,1)S(1)} custom-call(bf16[256,512]{1,0:T(8,128)(2,1)} %q_hbm.1, bf16[256,512]{1,0:T(8,128)(2,1)} %p_hbm.1, f32[512,512]{1,0:T(8,128)} %ce_hbm.1, f32[512,512]{1,0:T(8,128)} %cb_hbm.1, s32[1,512]{1,0:T(1,128)} %bitcast.2, s32[1,512]{1,0:T(1,128)} %bitcast.3), custom_call_target="tpu_custom_call" | custom-call | tf_op jit(solution)/shard_map/pallas_call | solution.py:505
  67.1 0.8 %fusion = (bf16[256,512]{1,0:T(8,128)(2,1)}, bf16[256,512]{1,0:T(8,128)(2,1)}) fusion(bf16[512,512]{1,0:T(8,128)(2,1)S(1)} %shard_map.77), kind=kLoop, calls=%fused_computation | loop fusion | bytes 1048576 | tf_op jit(solution)/shard_map/slice | solution.py:542

commit v3 on v2

--- a/solution.py
+++ b/solution.py
@@ -260,7 +260,7 @@
             ref[col, pl.ds(k, 1), :] = top[:, k * 128:(k + 1) * 128]
             ref[col, pl.ds(4 + k, 1), :] = total[:, k * 128:(k + 1) * 128]
 
-    def send_stats(ref, which):
+    def send_stats(ref, which, lo, hi):
         def body(j, carry):
             k = 8 + ((j + 1) // 2) * (1 - 2 * (j % 2))
             to = (col + k) % 16
@@ -269,7 +269,7 @@
             ).start()
             return carry
 
-        lax.fori_loop(0, 15, body, 0)
+        lax.fori_loop(lo, hi, body, 0)
 
     def wait_stats(ref, which):
         def body(k, carry):
@@ -327,7 +327,7 @@
             t_total = exp_sum(t_acc, t_top, 1.0)
             put_stats(st_t, t_top, t_total)
         if t == last_step:
-            send_stats(st_t, 1)
+            send_stats(st_t, 1, 0, 3)
         if t == last_step:
             assert p_steps[4] == z_steps[4] + 1 == t > max(p_steps[:4] + p_steps[5:] + z_steps)
             first, second = row_from((2, 2)), z_at(4) * 2 + 1 - core
@@ -349,7 +349,8 @@
     s_top = jnp.max(s_top, axis=0, keepdims=True)
     s_total = exp_sum(s_acc, s_top, 20.0)
     put_stats(st_s, s_top, s_total)
-    send_stats(st_s, 0)
+    send_stats(st_s, 0, 0, 15)
+    send_stats(st_t, 1, 3, 15)
 
     wait_stats(st_t, 1)
     t_scale = combine(st_t, 1.0) * -20.0

time: 68 us -> 68.2 us (level)
  no operation moved by 1% of the time
where the time goes in v3:
time: 68.2 us; the launch traced here: 68.1 us
  Pallas kernels  66.7 us (98%)
  local copies, waits for them, and re-layouts  0.82 us (1%)
    pallas_call x1, Pallas kernels, per_device(): pl.pallas_call(kernel, out_shape=out, in_specs=[hbm] * 6, out_specs=vmem,...  66.7 us

profile of v3, /device:TPU:1, one launch (start us, length us, event | category | flops | bytes accessed | tf_op | source)
XLA Modules:
  0.0 68.1 jit_solution(13220270765867953671)
XLA Ops:
  0.6 66.7 %shard_map.77 = bf16[512,512]{1,0:T(8,128)(2,1)S(1)} custom-call(bf16[256,512]{1,0:T(8,128)(2,1)} %q_hbm.1, bf16[256,512]{1,0:T(8,128)(2,1)} %p_hbm.1, f32[512,512]{1,0:T(8,128)} %ce_hbm.1, f32[512,512]{1,0:T(8,128)} %cb_hbm.1, s32[1,512]{1,0:T(1,128)} %bitcast.2, s32[1,512]{1,0:T(1,128)} %bitcast.3), custom_call_target="tpu_custom_call" | custom-call | tf_op jit(solution)/shard_map/pallas_call | solution.py:506
  67.3 0.8 %fusion = (bf16[256,512]{1,0:T(8,128)(2,1)}, bf16[256,512]{1,0:T(8,128)(2,1)}) fusion(bf16[512,512]{1,0:T(8,128)(2,1)S(1)} %shard_map.77), kind=kLoop, calls=%fused_computation | loop fusion | bytes 1048576 | tf_op jit(solution)/shard_map/slice | solution.py:543
